TPU v7x, 32 devices: a whole 2x2x4 slice. The times are simulated.
32 devices in a mesh: runs: 2 (over x), modes: 16 (over z, y, core).
Axes of the slice: x: 2, y: 2, z: 4, core: 2. Of those that a mesh axis runs over, the one named last changes fastest.
Arguments:
- amplitudes: float32 [8192, 2, 5, 512], P(('runs', 'modes')), parts along dimension 0, may hold values from -6 to 6
- mode_table: int32 [4096, 2], replicated, may hold values from 0 to 127, as said below
- slab_map: int32 [8], replicated, may hold values from 0 to 7, each once
- base_flow: float32 [1024], P('runs'), parts along dimension 0, may hold values from 0 to 1.5
- base_coupling: float32 [50, 512], P('runs'), parts along dimension 0, may hold values from -0.36 to 0.36
- slab_inverse: float32 [8, 64, 64], replicated
- wall_operator: float32 [64, 64], replicated, may hold values from -0.75 to 0.75
Outputs:
- marched: float32 [8192, 2, 5, 512], P(('runs', 'modes')), parts along dimension 0
There are 2 independent parts, one for each index of `runs`. A program takes and returns all parts, laid end to end along the dimension named above; an argument that names none is the same for every part. Nothing has to cross between parts.
Inputs may be any that keep to these rules, and one draw needn't show every extreme that they name: `mode_table`: every cell of the 32 x 128 grid is named by exactly one mode; column 0 lies in 0 to 31. `slab_map`: each subdomain has its own slot.
All inputs are finite; a program needn't handle non-finite values.
Results may differ from a plain program's by a relative error of at most 0.0003.
Values sent between devices are 32-bit elements; how exact they have to be, the bound alone decides.
No kernel may reach another device: no remote copies, remote signals or barrier semaphores. Data moves between devices by JAX's collectives and lax.ppermute only.
A program may use at most 192 MiB of HBM per device.

v0:
```python
import math
import jax
import jax.numpy as jnp
from jax import lax
from jax.sharding import PartitionSpec as P

M = 4096
NB = 128
SWEEPS = 3
NW = 32
precise = lax.Precision.HIGHEST
omega_step = 0.01
phase_gain = 0.2
march_step = 0.2
coupling = 0.3


def twiddle(length):
    counter = jnp.arange(length, dtype=jnp.int32)
    product = counter[:, None] * counter[None, :] % length
    angles = product.astype(jnp.float32) * (2.0 * math.pi / length)
    return (jnp.cos(angles), jnp.sin(angles))


def mode_tables(mode_table):
    omega_index = mode_table[:, 0]
    beta_index = mode_table[:, 1]
    signed = jnp.where(beta_index >= NB // 2, beta_index - NB, beta_index)
    wavenum = 2.0 * signed.astype(jnp.float32) / NB
    frequency = omega_step * omega_index.astype(jnp.float32)
    grid_pos = omega_index * NB + beta_index
    mode_at = jnp.zeros((M,), jnp.int32).at[grid_pos].set(jnp.arange(M, dtype=jnp.int32))
    return (wavenum, frequency, grid_pos, mode_at)


def synthesize(real_part, imag_part, tables, factor):
    cos_omega, sin_omega, cos_beta, sin_beta = tables
    mixed_re = jnp.einsum("...wb,bz->...wz", real_part, cos_beta, precision=precise) - jnp.einsum(
        "...wb,bz->...wz", imag_part, sin_beta, precision=precise
    )
    mixed_im = jnp.einsum("...wb,bz->...wz", real_part, sin_beta, precision=precise) + jnp.einsum(
        "...wb,bz->...wz", imag_part, cos_beta, precision=precise
    )
    physical = jnp.einsum("...wz,wt->...tz", mixed_re, cos_omega, precision=precise) - jnp.einsum(
        "...wz,wt->...tz", mixed_im, sin_omega, precision=precise
    )
    return physical * factor


def analyze(physical, tables, factor):
    cos_omega, sin_omega, cos_beta, sin_beta = tables
    half_re = jnp.einsum("...tz,zb->...tb", physical, cos_beta, precision=precise)
    half_im = -jnp.einsum("...tz,zb->...tb", physical, sin_beta, precision=precise)
    coef_re = jnp.einsum("...tb,tw->...wb", half_re, cos_omega, precision=precise) + jnp.einsum(
        "...tb,tw->...wb", half_im, sin_omega, precision=precise
    )
    coef_im = jnp.einsum("...tb,tw->...wb", half_im, cos_omega, precision=precise) - jnp.einsum(
        "...tb,tw->...wb", half_re, sin_omega, precision=precise
    )
    return (coef_re * factor, coef_im * factor)


def forcing(normal_vel, spanwise_vel, wall_grad, span_grad, tables, factor):
    vel_v = synthesize(normal_vel[0], normal_vel[1], tables, factor)
    vel_w = synthesize(spanwise_vel[0], spanwise_vel[1], tables, factor)
    grad_y = synthesize(wall_grad[0], wall_grad[1], tables, factor)
    grad_z = synthesize(span_grad[0], span_grad[1], tables, factor)
    product = -(vel_v[None] * grad_y + vel_w[None] * grad_z)
    return analyze(product, tables, factor)


def wall_derivative(values, wall_operator):
    slab_width = wall_operator.shape[0]
    slab_count = values.shape[3] // slab_width
    blocks = values.reshape(values.shape[:3] + (slab_count, slab_width))
    return jnp.einsum("ij,abcsj->abcsi", wall_operator, blocks, precision=precise).reshape(
        values.shape
    )


def interface_table(slab_map, slab_count, slab_width):
    inverse = (
        jnp.zeros((slab_count,), jnp.int32)
        .at[slab_map]
        .set(jnp.arange(slab_count, dtype=jnp.int32))
    )
    position = jnp.arange(slab_count * slab_width, dtype=jnp.int32)
    slot_of = position // slab_width
    within = position % slab_width
    domain = inverse[slot_of]
    below = slab_map[jnp.maximum(domain - 1, 0)] * slab_width + (slab_width - 1)
    above = slab_map[jnp.minimum(domain + 1, slab_count - 1)] * slab_width
    lower_ok = (within == 0) & (domain > 0)
    upper_ok = (within == slab_width - 1) & (domain < slab_count - 1)
    source = jnp.where(lower_ok, below, jnp.where(upper_ok, above, 0))
    weight = (lower_ok | upper_ok).astype(jnp.float32)
    return (source, weight)


def relaxation(iterate, right_side, rotation, matrix, slab_inverse, source, weight):
    slab_count = slab_inverse.shape[0]
    slab_width = slab_inverse.shape[1]
    coupled = jnp.einsum("kjy,acjy->acky", matrix, iterate, precision=precise)
    applied = jnp.stack(
        [
            coupled[:, 0] - rotation[:, None, :] * iterate[:, 1],
            coupled[:, 1] + rotation[:, None, :] * iterate[:, 0],
        ],
        1,
    )
    rims = jnp.take(iterate, source, axis=3) * weight
    residual_in = right_side - applied + coupling * rims
    blocks = residual_in.reshape(iterate.shape[:3] + (slab_count, slab_width))
    return jnp.einsum("sij,acvsj->acvsi", slab_inverse, blocks, precision=precise).reshape(
        iterate.shape
    )


def local(amplitudes, mode_table, slab_map, base_flow, base_coupling, slab_inverse, wall_operator):
    local_modes = amplitudes.shape[0]
    wall_points = amplitudes.shape[3]
    groups = lax.axis_size("modes")
    point_share = wall_points // groups
    wavenum, frequency, grid_pos, mode_at = mode_tables(mode_table)
    first_mode = lax.axis_index("modes") * local_modes
    wave_local = lax.dynamic_slice_in_dim(wavenum, first_mode, local_modes)
    freq_local = lax.dynamic_slice_in_dim(frequency, first_mode, local_modes)
    tables = twiddle(NW) + twiddle(NB)
    factor = 1.0 / math.sqrt(M)
    source, weight = interface_table(slab_map, slab_inverse.shape[0], slab_inverse.shape[1])
    matrix = base_coupling.reshape(5, 5, wall_points)
    gradient = wall_derivative(amplitudes, wall_operator)
    span = jnp.stack(
        [
            -wave_local[:, None, None] * amplitudes[:, 1],
            wave_local[:, None, None] * amplitudes[:, 0],
        ],
        1,
    )
    fields = jnp.concatenate([amplitudes[:, :, 2:4], gradient, span], 2)
    field_count = fields.shape[2]
    channels = 2 * field_count
    outgoing = jnp.transpose(
        fields.reshape(local_modes, channels, groups, point_share), (1, 2, 3, 0)
    ).reshape(channels, groups, point_share * local_modes)
    incoming = lax.all_to_all(outgoing, "modes", split_axis=1, concat_axis=1, tiled=True)
    by_mode = jnp.transpose(
        incoming.reshape(channels, groups, point_share, local_modes), (0, 2, 1, 3)
    ).reshape(channels, point_share, M)
    gridded = by_mode[..., mode_at].reshape(2, field_count, point_share, NW, NB)
    normal_vel = gridded[:, 0]
    spanwise_vel = gridded[:, 1]
    wall_grad = gridded[:, 2:7]
    span_grad = gridded[:, 7:12]
    mean_crossflow = lax.all_gather(spanwise_vel[0, :, 0, 0], "modes", axis=0, tiled=True)
    coef_re, coef_im = forcing(normal_vel, spanwise_vel, wall_grad, span_grad, tables, factor)
    packed = jnp.stack([coef_re, coef_im], 0).reshape(10, point_share, M)[..., grid_pos]
    sendback = jnp.transpose(
        packed.reshape(10, point_share, groups, local_modes), (0, 2, 1, 3)
    ).reshape(10, groups, point_share * local_modes)
    returned = lax.all_to_all(sendback, "modes", split_axis=1, concat_axis=1, tiled=True)
    nonlinear = jnp.transpose(
        returned.reshape(10, groups, point_share, local_modes), (3, 0, 1, 2)
    ).reshape(local_modes, 2, 5, wall_points)
    crossflow = base_flow + mean_crossflow
    rotation = phase_gain * wave_local[:, None] * crossflow[None, :] - freq_local[:, None]
    right_side = amplitudes + march_step * nonlinear
    iterate = amplitudes
    for sweep_index in range(SWEEPS):
        iterate = relaxation(iterate, right_side, rotation, matrix, slab_inverse, source, weight)
    return iterate


def solution(mesh):
    return jax.shard_map(
        local,
        mesh=mesh,
        in_specs=(
            P(("runs", "modes"), None, None, None),
            P(),
            P(),
            P("runs"),
            P("runs", None),
            P(),
            P(),
        ),
        out_specs=P(("runs", "modes"), None, None, None),
        check_vma=False,
    )
```

profile of v0, /device:TPU:16, one launch (start us, length us, event | category | flops | bytes accessed | tf_op | source)
XLA Modules:
  0.0 1126.5 jit_solution(16035738039939335785)
XLA Ops:
  0.0 9.0 copy.115
  9.0 8.7 copy.102
  19.0 4.6 slice.154
  23.6 4.1 slice_multiply_fusion.5
  27.8 5.3 fusion.90
  36.3 7.8 maximum_maximum_fusion
  44.1 17.6 %copy.106 = f32[256,2,12,512]{0,3,2,1:T(8,128)} copy(f32[256,2,12,512]{0,2,1,3:T(8,128)} %maximum_maximum_fusion) | data formatting | bytes 25165824 | tf_op jit(solution)/shard_map/concatenate | solution.py:140
  61.7 14.2 %reshape.217 = f32[24,16,8192]{2,1,0:T(8,128)} reshape(f32[24,16,32,256]{3,2,1,0:T(8,128)} %bitcast.293) | data formatting | bytes 25165824 | tf_op jit(solution)/shard_map/reshape | solution.py:145
  75.9 16.4 %copy.107 = f32[24,16,8192]{2,0,1:T(8,128)} copy(f32[24,16,8192]{2,1,0:T(8,128)} %reshape.217) | data formatting | bytes 25165824 | tf_op jit(solution)/shard_map/reshape | solution.py:145
  92.3 6.2 all-to-all-start
  98.4 15.7 %scatter_custom_fusion = s32[4096]{0:T(1024)S(1)} fusion(s32[4096]{0:T(1024)S(1)} %bitcast.308, s32[4096]{0:T(1024)S(1)} %iota.30, s32[]{:T(128)} %constant.98.clone.1), kind=kCustom, calls=%fused_computation.165 | custom fusion | bytes 16388 | tf_op jit(solution)/shard_map/scatter | solution.py:32
  114.2 256.7 %all-to-all-done = f32[24,16,8192]{2,0,1:T(8,128)} async-done(((f32[24,16,8192]{2,0,1:T(8,128)}), f32[24,16,8192]{2,0,1:T(8,128)}, u32[]{:S(2)}, u32[]{:S(2)}) %all-to-all-start) | async-done | bytes 12582944 | tf_op jit(solution)/shard_map/all_to_all | solution.py:146
  370.9 14.6 %copy.146 = f32[48,8,32,256]{3,2,1,0:T(8,128)} copy(f32[48,8,32,256]{3,1,2,0:T(8,128)} %bitcast.101) | data formatting | bytes 25165824
  385.5 29.6 %copy.138 = f32[24,32,16,256]{1,0,3,2:T(8,128)} copy(f32[24,32,16,256]{3,1,0,2:T(8,128)} %bitcast.294) | data formatting | bytes 25165824 | tf_op jit(solution)/shard_map/reshape | solution.py:149
  415.1 86.4 %gather_fusion = f32[4096,24,32]{2,1,0:T(8,128)} fusion(f32[24,32,4096]{1,0,2:T(8,128)} %bitcast.291, s32[4096]{0:T(1024)S(1)} %fusion.115), kind=kCustom, calls=%fused_computation.3 | custom fusion | bytes 25182208 | tf_op jit(solution)/shard_map/gather | solution.py:150
  501.5 32.3 %copy.110 = f32[24,32,4096]{2,1,0:T(8,128)} copy(f32[24,32,4096]{1,0,2:T(8,128)} %bitcast.292) | data formatting | bytes 25165824 | tf_op jit(solution)/shard_map/gather | solution.py:150
  533.8 12.0 %copy.147 = f32[96,8,32,128]{3,2,1,0:T(8,128)} copy(f32[96,8,32,128]{3,1,2,0:T(8,128)} %bitcast.295) | data formatting | bytes 25165824
  554.0 4.3 fusion.26
  558.2 4.3 fusion.28
  592.3 3.5 fusion.17
  614.5 6.8 reshape.221
  621.3 22.0 %copy.111 = f32[10,32,4096]{1,0,2:T(8,128)} copy(f32[10,32,4096]{2,1,0:T(8,128)} %reshape.221) | data formatting | bytes 10485760 | tf_op jit(solution)/shard_map/reshape | solution.py:157
  643.3 78.3 %gather_fusion.1 = f32[4096,10,32]{2,1,0:T(8,128)} fusion(f32[10,32,4096]{1,0,2:T(8,128)} %copy.111, s32[4096]{0:T(1024)S(1)} %broadcast_clamp_fusion), kind=kCustom, calls=%fused_computation.4 | custom fusion | bytes 10502144 | tf_op jit(solution)/shard_map/gather | solution.py:157
  721.6 21.3 %copy.112 = f32[10,32,16,256]{3,1,2,0:T(8,128)} copy(f32[10,32,16,256]{1,0,3,2:T(8,128)} %bitcast.296) | data formatting | bytes 10485760 | tf_op jit(solution)/shard_map/reshape | solution.py:159
  743.0 6.9 reshape.223
  749.9 9.0 copy.113
  758.9 4.8 all-to-all-start.1
  765.0 4.4 compare_select_fusion.10
  770.8 4.4 compare_select_fusion.4
  775.2 5.8 compare_and_fusion
  781.0 7.8 gather_fusion.2
  791.6 11.8 %convolution_bitcast_fusion.2 = f32[256,2,5,512]{0,2,1,3:T(8,128)} fusion(f32[256,2,5,512]{0,2,1,3:T(8,128)} %copy.115, f32[5,5,512,1]{1,0,3,2:T(8,128)S(1)} %copy.134), kind=kOutput, calls=%fused_computation.43 | convolution fusion | flops 78643200 | bytes 10536960 | tf_op jit(solution)/shard_map/kjy,acjy->acky/dot_general | solution.py:103
  805.3 159.1 %all-reduce = f32[512]{0:T(512)S(1)} all-reduce(f32[512]{0:T(512)S(1)} %dynamic-update-slice), channel_id=2, replica_groups=mesh['runs'=2,'modes'=16] {'modes'}, use_global_device_ids=true, to_apply=%add | all-reduce | flops 512 | bytes 4096 | tf_op jit(solution)/shard_map/all_gather | solution.py:155
  965.3 10.0 slice_subtract_fusion
  975.3 6.8 copy_multiply_fusion
  986.9 11.0 fusion
  997.9 8.4 fusion.38
  1012.8 9.8 convolution_bitcast_fusion.1
  1022.6 7.8 gather_fusion.3
  1030.4 8.8 fusion.15
  1041.6 10.4 fusion.1
  1052.0 8.4 fusion.41
  1066.9 9.9 convolution_bitcast_fusion
  1076.8 7.9 gather_fusion.4
  1084.6 8.7 fusion.13
  1095.7 10.5 fusion.2
  1106.1 8.4 fusion.44
  1117.2 8.8 copy.128
  (110 shorter events, 93.7 us)
Async XLA Ops:
  0.0 997.9 %copy-start = (f32[8,64,64]{2,1,0:T(8,128)S(1)}, f32[8,64,64]{2,1,0:T(8,128)}, u32[]{:S(2)}) copy-start(f32[8,64,64]{2,1,0:T(8,128)} %param.14) | copy-start | bytes 393220
  9.0 8.7 copy-start.13
  19.0 8.8 slice-start.4
  23.6 4.1 slice-start.5
  23.6 4.1 copy-start.12
  92.3 278.6 %all-to-all-start = ((f32[24,16,8192]{2,0,1:T(8,128)}), f32[24,16,8192]{2,0,1:T(8,128)}, u32[]{:S(2)}, u32[]{:S(2)}) async-start(f32[24,16,8192]{2,0,1:T(8,128)} %copy.107), calls=%async_computation | async-start | bytes 25165824 | tf_op jit(solution)/shard_map/all_to_all | solution.py:146
  547.7 14.8 %copy-start.3 = (f32[96,8,32,128]{3,2,1,0:T(8,128)S(1)}, f32[96,8,32,128]{3,2,1,0:T(8,128)}, u32[]{:S(2)}) copy-start(f32[96,8,32,128]{3,2,1,0:T(8,128)} %copy.147) | copy-start | bytes 37748740
  758.8 4.8 copy-start.14
  758.9 216.5 %all-to-all-start.1 = ((f32[10,16,8192]{2,0,1:T(8,128)}), f32[10,16,8192]{2,0,1:T(8,128)}, u32[]{:S(2)}, u32[]{:S(2)}) async-start(f32[10,16,8192]{2,0,1:T(8,128)} %copy.113), calls=%async_computation.1 | async-start | bytes 16777216 | tf_op jit(solution)/shard_map/all_to_all | solution.py:161
  781.0 7.8 copy-start.11
  781.0 8.6 copy-start.17
  791.6 172.8 %copy-start.16 = (f32[512]{0:T(512)S(1)}, f32[512]{0:T(512)}, u32[]{:S(2)}) copy-start(f32[512]{0:T(512)} %param.12) | copy-start | bytes 6148
  791.6 172.8 %copy-start.15 = (f32[256]{0:T(256)S(1)}, f32[256]{0:T(256)}, u32[]{:S(2)}) copy-start(f32[256]{0:T(256)} %get-tuple-element.8) | copy-start | bytes 3076
  964.5 0.9 copy-start.9
  982.1 2.2 copy-start.7
  982.1 4.8 copy-start.8
  984.0 14.0 %copy-start.4 = (f32[20,8,32,256]{3,2,1,0:T(8,128)}, f32[20,8,32,256]{3,2,1,0:T(8,128)S(1)}, u32[]{:S(2)}) copy-start(f32[20,8,32,256]{3,2,1,0:T(8,128)S(1)} %copy.148) | copy-start | bytes 15728644
  1009.5 3.3 copy-start.2
  1022.6 16.6 %slice-start = ((s8[5242880]{0:T(1024)(128)(4,1)}), s8[1048576]{0:T(1024)(128)(4,1)S(1)}, s32[]{:S(2)}) async-start(s8[5242880]{0:T(1024)(128)(4,1)} %bitcast.285), calls=%async_computation.2 | async-start | bytes 2097152
  1030.4 8.8 slice-start.1
  1030.4 11.2 copy-start.6
  1063.6 3.3 copy-start.1
  1076.7 7.9 copy-start.10
  1076.7 16.6 %slice-start.2 = ((s8[5242880]{0:T(1024)(128)(4,1)}), s8[1048576]{0:T(1024)(128)(4,1)S(1)}, s32[]{:S(2)}) async-start(s8[5242880]{0:T(1024)(128)(4,1)} %bitcast.288), calls=%async_computation.4 | async-start | bytes 2097152
  1084.6 8.7 slice-start.3
  1084.6 11.0 copy-start.5
where the time goes:
time: 1140 us; the launch traced here: 1130 us
  local copies, waits for them, and re-layouts  472 us (41%)
  waiting for transfers between devices  257 us (23%)
  blocking collectives  159 us (14%)
  matrix products  127 us (11%)
  other arithmetic  98.3 us (9%)
    all_to_all x1, waiting for transfers between devices, local(): lax.all_to_all(outgoing, 'modes', split_axis=1, concat_axis=1, tiled=True)  257 us
    all_gather x1, blocking collectives, local(): lax.all_gather(spanwise_vel[0, :, 0, 0], 'modes', axis=0, tiled=True)  159 us
    gather x2, local copies, waits for them, and re-layouts, local(): gridded = by_mode[..., mode_at].reshape(2, field_count, point_share, NW, NB)  119 us
    gather x1, local copies, waits for them, and re-layouts, local(): jnp.stack([coef_re, coef_im], 0).reshape(10, point_share, M)[..., grid_pos]  78.3 us
    unnamed x56, local copies, waits for them, and re-layouts  62 us
    add x3, other arithmetic, relaxation(): residual_in = right_side - applied + coupling * rims  31.9 us
    dot_general x3, matrix products, relaxation(): coupled = jnp.einsum('kjy,acjy->acky', matrix, iterate, precision=precise)  31.5 us
    reshape x2, local copies, waits for them, and re-layouts, local(): outgoing = jnp.transpose(fields.reshape(local_modes, channels, groups, po...  30.6 us
  transfers between devices with their start and end apart: 2, of which 1 were waited for; matrix products, arithmetic and copies ran while one was open for 6% of the time, Pallas kernels for 0%

commit v1 on v0

--- a/solution.py
+++ b/solution.py
@@ -143,7 +143,12 @@
     outgoing = jnp.transpose(
         fields.reshape(local_modes, channels, groups, point_share), (1, 2, 3, 0)
     ).reshape(channels, groups, point_share * local_modes)
-    incoming = lax.all_to_all(outgoing, "modes", split_axis=1, concat_axis=1, tiled=True)
+    incoming = jnp.concatenate(
+        lax.all_to_all(
+            jnp.stack(jnp.split(outgoing, lax.axis_size("modes"), axis=1)), "modes", 0, 0
+        ),
+        axis=1,
+    )
     by_mode = jnp.transpose(
         incoming.reshape(channels, groups, point_share, local_modes), (0, 2, 1, 3)
     ).reshape(channels, point_share, M)

time: 1140 us -> 1240 us (1.088)
  local copies, waits for them, and re-layouts: 472 us -> 567 us
    unnamed x56 -> x71, local copies, waits for them, and re-layouts: 62 us -> 130 us
    reshape x0 -> x1, local copies, waits for them, and re-layouts: none -> 38.7 us  [local(): jnp.concatenate(lax.all_to_all(jnp.stack(jnp.split(outgoing, lax.axis_siz...]
    reshape x2 -> x1, local copies, waits for them, and re-layouts: 30.6 us -> 14.2 us  [local(): outgoing = jnp.transpose(fields.reshape(local_modes, channels, groups, po...]
  transfers between devices with their start and end apart: 2 -> 2, of which waited for: 1 -> 1; matrix products, arithmetic and copies ran while one was open for 6% -> 5% of each run, Pallas kernels for 0% -> 0%
where the time goes in v1:
time: 1240 us; the launch traced here: 1220 us
  local copies, waits for them, and re-layouts  567 us (46%)
  waiting for transfers between devices  257 us (21%)
  blocking collectives  159 us (13%)
  matrix products  127 us (10%)
  other arithmetic  98.2 us (8%)
    all_to_all x1, waiting for transfers between devices, local(): lax.all_to_all(jnp.stack(jnp.split(outgoing, lax.axis_size('modes'), axis...  257 us
    all_gather x1, blocking collectives, local(): lax.all_gather(spanwise_vel[0, :, 0, 0], 'modes', axis=0, tiled=True)  159 us
    unnamed x71, local copies, waits for them, and re-layouts  130 us
    gather x2, local copies, waits for them, and re-layouts, local(): gridded = by_mode[..., mode_at].reshape(2, field_count, point_share, NW, NB)  119 us
    gather x1, local copies, waits for them, and re-layouts, local(): jnp.stack([coef_re, coef_im], 0).reshape(10, point_share, M)[..., grid_pos]  78.3 us
    reshape x1, local copies, waits for them, and re-layouts, local(): jnp.concatenate(lax.all_to_all(jnp.stack(jnp.split(outgoing, lax.axis_siz...  38.7 us
    add x3, other arithmetic, relaxation(): residual_in = right_side - applied + coupling * rims  31.9 us
    dot_general x3, matrix products, relaxation(): coupled = jnp.einsum('kjy,acjy->acky', matrix, iterate, precision=precise)  31.5 us
  transfers between devices with their start and end apart: 2, of which 1 were waited for; matrix products, arithmetic and copies ran while one was open for 5% of the time, Pallas kernels for 0%

profile of v1, /device:TPU:16, one launch (start us, length us, event | category | flops | bytes accessed | tf_op | source)
XLA Modules:
  0.0 1221.4 jit_solution(16425496656666335703)
XLA Ops:
  0.0 9.0 copy.113
  9.0 8.7 copy.101
  19.0 4.6 slice.154
  27.8 5.3 fusion.106
  36.4 7.7 maximum_maximum_fusion
  44.1 17.6 %copy.105 = f32[256,2,12,512]{0,3,2,1:T(8,128)} copy(f32[256,2,12,512]{0,2,1,3:T(8,128)} %maximum_maximum_fusion) | data formatting | bytes 25165824 | tf_op jit(solution)/shard_map/concatenate | solution.py:140
  61.7 14.2 %reshape.217 = f32[24,16,8192]{2,1,0:T(8,128)} reshape(f32[24,16,32,256]{3,2,1,0:T(8,128)} %bitcast.359) | data formatting | bytes 25165824 | tf_op jit(solution)/shard_map/reshape | solution.py:145
  84.6 4.6 fusion.70
  89.2 4.6 fusion.69
  103.0 4.6 fusion.66
  125.4 4.6 fusion.61
  134.6 4.6 fusion.59
  143.7 4.7 fusion.57
  148.4 6.5 all-to-all-start
  154.9 15.5 %scatter_custom_fusion = s32[4096]{0:T(1024)S(1)} fusion(s32[4096]{0:T(1024)S(1)} %bitcast.375, s32[4096]{0:T(1024)S(1)} %iota.30, s32[]{:T(128)} %constant.98.clone.1), kind=kCustom, calls=%fused_computation.198 | custom fusion | bytes 16388 | tf_op jit(solution)/shard_map/scatter | solution.py:32
  170.4 256.7 %all-to-all-done = f32[16,24,1,8192]{3,2,1,0:T(1,128)} async-done(((f32[16,24,1,8192]{3,2,1,0:T(1,128)}), f32[16,24,1,8192]{3,2,1,0:T(1,128)}, u32[]{:S(2)}, u32[]{:S(2)}) %all-to-all-start) | async-done | bytes 12582944 | tf_op jit(solution)/shard_map/all_to_all | solution.py:147
  427.2 38.7 %bitcast_reduce_fusion = f32[24,16,8192]{2,0,1:T(8,128)} fusion(f32[16,24,1,8192]{3,2,1,0:T(1,128)} %all-to-all-done), kind=kLoop, calls=%fused_computation.8 | loop fusion | bytes 25165824 | tf_op jit(solution)/shard_map/reshape | solution.py:146
  465.9 14.6 %copy.144 = f32[48,8,32,256]{3,2,1,0:T(8,128)} copy(f32[48,8,32,256]{3,1,2,0:T(8,128)} %bitcast.360) | data formatting | bytes 25165824
  480.5 29.6 %copy.136 = f32[24,32,16,256]{1,0,3,2:T(8,128)} copy(f32[24,32,16,256]{3,1,0,2:T(8,128)} %bitcast.361) | data formatting | bytes 25165824 | tf_op jit(solution)/shard_map/reshape | solution.py:154
  510.1 86.3 %gather_fusion = f32[4096,24,32]{2,1,0:T(8,128)} fusion(f32[24,32,4096]{1,0,2:T(8,128)} %bitcast.357, s32[4096]{0:T(1024)S(1)} %get-tuple-element.38), kind=kCustom, calls=%fused_computation.3 | custom fusion | bytes 25182208 | tf_op jit(solution)/shard_map/gather | solution.py:155
  596.4 32.3 %copy.108 = f32[24,32,4096]{2,1,0:T(8,128)} copy(f32[24,32,4096]{1,0,2:T(8,128)} %bitcast.358) | data formatting | bytes 25165824 | tf_op jit(solution)/shard_map/gather | solution.py:155
  628.7 12.0 copy.145
  709.4 6.8 reshape.221
  716.3 22.0 %copy.109 = f32[10,32,4096]{1,0,2:T(8,128)} copy(f32[10,32,4096]{2,1,0:T(8,128)} %reshape.221) | data formatting | bytes 10485760 | tf_op jit(solution)/shard_map/reshape | solution.py:162
  738.2 78.3 %gather_fusion.1 = f32[4096,10,32]{2,1,0:T(8,128)} fusion(f32[10,32,4096]{1,0,2:T(8,128)} %copy.109, s32[4096]{0:T(1024)S(1)} %get-tuple-element.39), kind=kCustom, calls=%fused_computation.4 | custom fusion | bytes 10502144 | tf_op jit(solution)/shard_map/gather | solution.py:162
  816.6 21.3 %copy.110 = f32[10,32,16,256]{3,1,2,0:T(8,128)} copy(f32[10,32,16,256]{1,0,3,2:T(8,128)} %bitcast.363) | data formatting | bytes 10485760 | tf_op jit(solution)/shard_map/reshape | solution.py:164
  837.9 6.9 reshape.223
  844.8 9.0 copy.111
  853.8 4.8 all-to-all-start.1
  870.9 5.7 compare_and_fusion
  876.7 7.8 gather_fusion.2
  886.3 11.8 convolution_bitcast_fusion.2
  900.0 159.2 %all-reduce = f32[512]{0:T(512)S(1)} all-reduce(f32[512]{0:T(512)S(1)} %dynamic-update-slice), channel_id=2, replica_groups=mesh['runs'=2,'modes'=16] {'modes'}, use_global_device_ids=true, to_apply=%add | all-reduce | flops 512 | bytes 4096 | tf_op jit(solution)/shard_map/all_gather | solution.py:160
  1060.3 10.0 slice_subtract_fusion
  1070.2 6.8 copy_multiply_fusion
  1081.8 11.0 fusion
  1092.9 8.4 fusion.38
  1107.7 9.8 convolution_bitcast_fusion.1
  1117.5 7.8 gather_fusion.3
  1125.4 8.8 fusion.15
  1136.5 10.4 fusion.1
  1146.9 8.4 fusion.41
  1161.8 9.9 convolution_bitcast_fusion
  1171.6 7.9 gather_fusion.4
  1179.5 8.7 fusion.13
  1190.5 10.5 fusion.2
  1201.0 8.4 fusion.44
  1212.1 8.8 copy.126
  (125 shorter events, 163.4 us)
Async XLA Ops:
  0.0 1092.9 %copy-start = (f32[8,64,64]{2,1,0:T(8,128)S(1)}, f32[8,64,64]{2,1,0:T(8,128)}, u32[]{:S(2)}) copy-start(f32[8,64,64]{2,1,0:T(8,128)} %param.14) | copy-start | bytes 393220
  9.0 8.7 copy-start.13
  19.0 8.8 slice-start.4
  23.6 4.1 slice-start.5
  23.6 4.1 copy-start.12
  148.4 278.8 %all-to-all-start = ((f32[16,24,1,8192]{3,2,1,0:T(1,128)}), f32[16,24,1,8192]{3,2,1,0:T(1,128)}, u32[]{:S(2)}, u32[]{:S(2)}) async-start(f32[16,24,1,8192]{3,2,1,0:T(1,128)} %fusion.57), calls=%async_computation | async-start | bytes 25165824 | tf_op jit(solution)/shard_map/all_to_all | solution.py:147
  640.7 16.7 %copy-start.3 = (f32[96,8,32,128]{3,2,1,0:T(8,128)S(1)}, f32[96,8,32,128]{3,2,1,0:T(8,128)}, u32[]{:S(2)}) copy-start(f32[96,8,32,128]{3,2,1,0:T(8,128)} %copy.145) | copy-start | bytes 37748740
  853.8 4.9 copy-start.11
  853.8 5.7 copy-start.14
  853.8 216.4 %all-to-all-start.1 = ((f32[10,16,8192]{2,0,1:T(8,128)}), f32[10,16,8192]{2,0,1:T(8,128)}, u32[]{:S(2)}, u32[]{:S(2)}) async-start(f32[10,16,8192]{2,0,1:T(8,128)} %copy.111), calls=%async_computation.1 | async-start | bytes 16777216 | tf_op jit(solution)/shard_map/all_to_all | solution.py:166
  876.6 7.8 copy-start.17
  886.3 172.9 %copy-start.16 = (f32[512]{0:T(512)S(1)}, f32[512]{0:T(512)}, u32[]{:S(2)}) copy-start(f32[512]{0:T(512)} %param.12) | copy-start | bytes 6148
  886.3 172.9 %copy-start.15 = (f32[256]{0:T(256)S(1)}, f32[256]{0:T(256)}, u32[]{:S(2)}) copy-start(f32[256]{0:T(256)} %get-tuple-element.8) | copy-start | bytes 3076
  1059.4 0.9 copy-start.9
  1077.0 2.2 copy-start.7
  1077.0 4.8 copy-start.8
  1078.9 14.0 %copy-start.4 = (f32[20,8,32,256]{3,2,1,0:T(8,128)}, f32[20,8,32,256]{3,2,1,0:T(8,128)S(1)}, u32[]{:S(2)}) copy-start(f32[20,8,32,256]{3,2,1,0:T(8,128)S(1)} %copy.146) | copy-start | bytes 15728644
  1104.4 3.3 copy-start.2
  1117.5 16.6 %slice-start = ((s8[5242880]{0:T(1024)(128)(4,1)}), s8[1048576]{0:T(1024)(128)(4,1)S(1)}, s32[]{:S(2)}) async-start(s8[5242880]{0:T(1024)(128)(4,1)} %bitcast.351), calls=%async_computation.2 | async-start | bytes 2097152
  1125.4 8.8 slice-start.1
  1125.4 11.2 copy-start.6
  1158.5 3.3 copy-start.1
  1171.6 7.9 copy-start.10
  1171.6 16.6 %slice-start.2 = ((s8[5242880]{0:T(1024)(128)(4,1)}), s8[1048576]{0:T(1024)(128)(4,1)S(1)}, s32[]{:S(2)}) async-start(s8[5242880]{0:T(1024)(128)(4,1)} %bitcast.354), calls=%async_computation.4 | async-start | bytes 2097152
  1179.5 8.7 slice-start.3
  1179.5 11.0 copy-start.5
